TPU v7x, 32 devices: a whole 2x2x4 slice. The times are simulated.
32 devices in a mesh: grp: 4 (over y, x), gx: 4 (over z), gy: 2 (over core).
Axes of the slice: x: 2, y: 2, z: 4, core: 2. Of those that a mesh axis runs over, the one named last changes fastest.
Arguments:
- coarse_modes: float32 [4, 2, 8, 32, 4096], P('grp', None, None, 'gy', 'gx'), may hold values from -6 to 6
- salinity: float32 [32, 128, 16384], P('grp', 'gy', 'gx'), may hold values from -6 to 6
- viscosity: float32 [4], P('grp'), may hold values from 0.1 to 1
- forcing_gain: float32 [4], P('grp'), may hold values from 0.5 to 2
- diffusivity: float32 [32], P('grp'), may hold values from 0.3 to 1.5
Outputs:
- salinity_next: float32 [32, 128, 16384], P('grp', 'gy', 'gx')
- coarse_next: float32 [4, 2, 8, 32, 4096], P('grp', None, None, 'gy', 'gx')
All inputs are finite; a program needn't handle non-finite values.
Results may differ from a plain program's by a relative error of at most 0.0003.
Values sent between devices are 32-bit elements; how exact they have to be, the bound alone decides.
A program may use at most 192 MiB of HBM per device.

v0:
```python
import math
import jax
import jax.numpy as jnp
from jax import lax
from jax.sharding import PartitionSpec as P

RATIO = 4
fine_step = 0.1


def extended(cells, sides, width):
    for axis, dim in sides:
        count = lax.axis_size(axis)
        head = lax.slice_in_dim(cells, 0, width, axis=dim)
        tail = lax.slice_in_dim(cells, cells.shape[dim] - width, cells.shape[dim], axis=dim)
        cells = jnp.concatenate(
            [
                lax.ppermute(tail, axis, [(i, (i + 1) % count) for i in range(count)]),
                cells,
                lax.ppermute(head, axis, [((i + 1) % count, i) for i in range(count)]),
            ],
            axis=dim,
        )
    return cells


def circle_table(row_count, col_count, period, orient):
    product = (
        lax.broadcasted_iota(jnp.int32, (row_count, col_count), 0)
        * lax.broadcasted_iota(jnp.int32, (row_count, col_count), 1)
        % period
    )
    angle = 2.0 * math.pi / period * product.astype(jnp.float32)
    return (jnp.cos(angle), orient * jnp.sin(angle))


def contract(data, table, form):
    return jnp.einsum(form, data, table, precision=lax.Precision.HIGHEST)


def fourier_lines(real_part, imag_part, orient, want_imag):
    length = real_part.shape[-1]
    exponent = length.bit_length() - 1
    inner_count = 2 ** ((exponent + 2) // 2)
    outer_count = length // inner_count
    leading = real_part.shape[:-1]
    cos_outer, sin_outer = circle_table(outer_count, outer_count, outer_count, orient)
    cos_twist, sin_twist = circle_table(outer_count, inner_count, length, orient)
    cos_inner, sin_inner = circle_table(inner_count, inner_count, inner_count, orient)
    first_form = "...ba,bk->...ka"
    second_form = "...ka,aj->...jk"
    split_real = real_part.reshape(leading + (outer_count, inner_count))
    section_real = contract(split_real, cos_outer, first_form)
    section_imag = contract(split_real, sin_outer, first_form)
    if imag_part is not None:
        split_imag = imag_part.reshape(leading + (outer_count, inner_count))
        section_real = section_real - contract(split_imag, sin_outer, first_form)
        section_imag = section_imag + contract(split_imag, cos_outer, first_form)
    twist_real = section_real * cos_twist - section_imag * sin_twist
    twist_imag = section_real * sin_twist + section_imag * cos_twist
    norm_factor = length ** (-0.5)
    final_real = (
        contract(twist_real, cos_inner, second_form) - contract(twist_imag, sin_inner, second_form)
    ) * norm_factor
    if not want_imag:
        return final_real.reshape(leading + (length,))
    final_imag = (
        contract(twist_real, sin_inner, second_form) + contract(twist_imag, cos_inner, second_form)
    ) * norm_factor
    return (final_real.reshape(leading + (length,)), final_imag.reshape(leading + (length,)))


def refine_rows(padded, dimension):
    extent = padded.shape[dimension] - 2
    middle = lax.slice_in_dim(padded, 1, extent + 1, axis=dimension)
    previous = lax.slice_in_dim(padded, 0, extent, axis=dimension)
    following = lax.slice_in_dim(padded, 2, extent + 2, axis=dimension)
    pieces = []
    for sub_cell in range(RATIO):
        offset = (sub_cell + 0.5) / RATIO - 0.5
        beside = following if offset > 0 else previous
        pieces.append((1.0 - abs(offset)) * middle + abs(offset) * beside)
    stacked = jnp.stack(pieces, axis=dimension + 1)
    target = list(middle.shape)
    target[dimension] = extent * RATIO
    return stacked.reshape(target)


def spread_table(cell_count):
    fine_count = cell_count * RATIO
    source = lax.broadcasted_iota(jnp.int32, (cell_count + 2, fine_count), 0)
    fine_cell = lax.broadcasted_iota(jnp.int32, (cell_count + 2, fine_count), 1)
    parent = fine_cell // RATIO
    sub_cell = (fine_cell % RATIO).astype(jnp.float32)
    offset = (sub_cell + 0.5) / RATIO - 0.5
    magnitude = jnp.abs(offset)
    own_weight = jnp.where(source == parent + 1, 1.0 - magnitude, 0.0)
    after_weight = jnp.where((source == parent + 2) & (offset > 0), magnitude, 0.0)
    before_weight = jnp.where((source == parent) & (offset < 0), magnitude, 0.0)
    return own_weight + after_weight + before_weight


def average_table(fine_count):
    fine_cell = lax.broadcasted_iota(jnp.int32, (fine_count, fine_count // RATIO), 0)
    coarse_cell = lax.broadcasted_iota(jnp.int32, (fine_count, fine_count // RATIO), 1)
    return jnp.where(fine_cell // RATIO == coarse_cell, 1.0 / RATIO, 0.0).astype(jnp.float32)


def per_device(coarse_modes, salinity, viscosity, forcing_gain, diffusivity):
    planes = coarse_modes.shape[2]
    row_count = coarse_modes.shape[3]
    width = coarse_modes.shape[4]
    groups = lax.axis_size("grp")
    quarter = planes // groups
    pencil = lax.all_to_all(coarse_modes[0], "gx", split_axis=2, concat_axis=3, tiled=True)
    physical = fourier_lines(pencil[0], pencil[1], 1.0, False)
    blocks = lax.all_to_all(physical, "gx", split_axis=2, concat_axis=1, tiled=True)
    received = lax.all_to_all(
        blocks.reshape(groups, quarter, row_count, width),
        "grp",
        split_axis=0,
        concat_axis=0,
        tiled=True,
    )
    rimmed = extended(received, (("gx", 3), ("gy", 2)), 1)
    along_y = refine_rows(rimmed, 2)
    velocity = jnp.einsum(
        "fqyj,jx->fqyx", along_y, spread_table(width), precision=lax.Precision.HIGHEST
    )[:, :, None]
    padded = extended(salinity, (("grp", 0), ("gx", 2), ("gy", 1)), 1)

    def levels(piece):
        return piece.reshape((quarter, RATIO) + piece.shape[1:])

    centre = levels(padded[1:-1, 1:-1, 1:-1])
    east_cells = levels(padded[1:-1, 1:-1, 2:])
    west_cells = levels(padded[1:-1, 1:-1, :-2])
    north_cells = levels(padded[1:-1, 2:, 1:-1])
    south_cells = levels(padded[1:-1, :-2, 1:-1])
    upper_cells = levels(padded[2:, 1:-1, 1:-1])
    lower_cells = levels(padded[:-2, 1:-1, 1:-1])
    diffuse_rate = diffusivity.reshape(quarter, RATIO, 1, 1)
    spread = diffuse_rate * (
        east_cells
        + west_cells
        + north_cells
        + south_cells
        + upper_cells
        + lower_cells
        - 6.0 * centre
    )
    advection = (
        velocity[0] * (east_cells - west_cells) * 0.5
        + velocity[1] * (north_cells - south_cells) * 0.5
        + velocity[2] * (upper_cells - lower_cells) * 0.5
    )
    updated = centre + fine_step * (spread - advection)
    buoyancy = velocity[3] - updated
    partial_mean = buoyancy.reshape(quarter, RATIO, row_count, RATIO, width * RATIO).mean(
        axis=(1, 3)
    )
    restricted = jnp.einsum(
        "qyx,xc->qyc", partial_mean, average_table(width * RATIO), precision=lax.Precision.HIGHEST
    )
    salinity_next = updated.reshape(salinity.shape)
    columns = lax.all_to_all(restricted, "gx", split_axis=1, concat_axis=2, tiled=True)
    spec_real, spec_imag = fourier_lines(columns, None, -1.0, True)
    own_spectra = lax.all_to_all(
        jnp.stack([spec_real, spec_imag]), "gx", split_axis=3, concat_axis=2, tiled=True
    )
    spectrum = lax.all_gather(own_spectra, "grp", axis=1, tiled=True)
    total_modes = width * lax.axis_size("gx")
    mode_index = lax.axis_index("gx") * width + lax.broadcasted_iota(jnp.int32, (width,), 0)
    wavenumber = jnp.where(mode_index < total_modes // 2, mode_index, mode_index - total_modes)
    scaled_wave = 2.0 * math.pi / total_modes * wavenumber.astype(jnp.float32)
    damping = jnp.exp(-viscosity[0] * scaled_wave * scaled_wave)
    coarse_next = damping * coarse_modes + forcing_gain[0] * spectrum[None]
    return (salinity_next, coarse_next)


def solution(mesh):
    return jax.shard_map(
        per_device,
        mesh=mesh,
        in_specs=(
            P("grp", None, None, "gy", "gx"),
            P("grp", "gy", "gx"),
            P("grp"),
            P("grp"),
            P("grp"),
        ),
        out_specs=(P("grp", "gy", "gx"), P("grp", None, None, "gy", "gx")),
        check_vma=False,
    )
```

profile of v0, /device:TPU:0, one launch (start us, length us, event | category | flops | bytes accessed | tf_op | source)
XLA Modules:
  0.0 611.9 jit_solution(15388535690880584705)
XLA Ops:
  10.0 6.3 %all-to-all-start = ((f32[2,8,16,1024]{3,1,0,2:T(8,128)}), f32[2,8,16,1024]{3,1,0,2:T(8,128)S(1)}, u32[]{:S(2)}, u32[]{:S(2)}) async-start(f32[2,8,16,1024]{3,1,0,2:T(8,128)} %bitcast.143), calls=%async_computation | async-start | bytes 2097152 | tf_op jit(solution)/shard_map/all_to_all | solution.py:115
  21.5 11.6 %copy.106 = f32[8,64,4096]{2,0,1:T(8,128)} copy(f32[8,64,4096]{2,1,0:T(8,128)} %param.6) | data formatting | bytes 16777216 | tf_op args[1]
  33.1 9.9 %reshape.129 = f32[2,4,16,4,4096]{4,3,2,1,0:T(4,128)} reshape(f32[8,64,4096]{2,1,0:T(8,128)} %param.6) | data formatting | bytes 16777216 | tf_op jit(solution)/shard_map/reshape | solution.py:133
  46.1 21.0 %collective-permute-done = f32[1,64,4096]{2,1,0:T(8,128)} collective-permute-done((f32[1,64,4096]{2,1,0:T(8,128)}, f32[1,64,4096]{2,1,0:T(8,128)}, u32[]{:S(2)}, u32[]{:S(2)}) %collective-permute-start) | collective-permute-done | bytes 1048608 | tf_op jit(solution)/shard_map/ppermute | solution.py:18
  78.7 7.5 %copy.128 = f32[8,4,128,32]{0,1,3,2:T(4,128)} copy(f32[8,4,128,32]{2,3,1,0:T(8,128)S(1)} %fusion.39) | data formatting | bytes 1048576 | tf_op jit(solution)/shard_map/reshape | solution.py:66
  86.2 12.1 %reshape.143 = f32[4,1,32768]{2,1,0:T(1,128)} reshape(f32[4096,4,8]{2,1,0:T(4,128)} %bitcast.148) | data formatting | bytes 1048576
  98.3 5.2 all-to-all-start.1
  103.5 5.6 pad_maximum_fusion
  109.2 5.8 copy-done
  116.1 3.8 collective-permute-start.2
  120.5 3.9 reduce
  124.4 14.3 %reshape.144 = f32[4096,4,8]{2,1,0:T(4,128)} reshape(f32[4,32768]{1,0:T(4,128)} %reduce) | data formatting | bytes 1048576
  138.7 7.7 %copy.99 = f32[8,4,4,1024]{3,2,1,0:T(4,128)} copy(f32[8,4,4,1024]{0,2,3,1:T(4,128)} %bitcast.149) | data formatting | bytes 1048576 | tf_op jit(solution)/shard_map/all_to_all | solution.py:117
  148.4 4.1 all-to-all-start.2
  152.5 8.8 %pad_maximum_fusion.2 = f32[8,64,4096]{2,0,1:T(8,128)} fusion(f32[1,64,4096]{2,0,1:T(1,128)S(1)} %copy.89, f32[8,64,4096]{2,0,1:T(8,128)} %copy.106), kind=kLoop, calls=%fused_computation.38 | loop fusion | flops 2097152 | bytes 17825792 | tf_op jit(solution)/shard_map/concatenate | solution.py:16
  161.3 9.8 %reshape.132 = f32[2,4,16,4,4096]{4,1,0,3,2:T(4,128)} reshape(f32[8,64,4096]{2,0,1:T(8,128)} %pad_maximum_fusion.2) | data formatting | bytes 16777216 | tf_op jit(solution)/shard_map/reshape | solution.py:133
  171.1 21.4 %concatenate.38 = f32[10,64,4098]{2,0,1:T(8,128)} concatenate(f32[10,64,1]{2,0,1:T(8,128)S(1)} %collective-permute-done.3, f32[10,64,4096]{2,0,1:T(8,128)} %copy-done, f32[10,64,1]{2,0,1:T(8,128)S(1)} %collective-permute-done.2), dimensions={2} | concatenate | bytes 20981760 | tf_op jit(solution)/shard_map/concatenate | solution.py:16
  193.7 3.7 collective-permute-start.7
  203.5 23.8 %fusion.36 = (f32[8,64,4096]{2,0,1:T(8,128)}, f32[8,64,4096]{2,0,1:T(8,128)}, f32[8,64,4096]{2,0,1:T(8,128)}) fusion(f32[10,64,1]{2,0,1:T(8,128)S(1)} %collective-permute-done.2, f32[1,64,4096]{2,0,1:T(1,128)S(1)} %copy.89, f32[8,64,4096]{2,0,1:T(8,128)} %copy.106, f32[1,64,4096]{2,0,1:T(1,128)S(1)} %copy.87, f32[10,64,1]{2,0,1:T(8,128)S(1)} %collective-permute-done.3), kind=kLoop, calls=%fused_computation.54 | loop fusion | flops 18874368 | bytes 35656704 | tf_op jit(solution)/shard_map/add | solution.py:144
  227.4 9.8 %add.235 = f32[2,4,16,4,4096]{4,1,0,3,2:T(4,128)} reshape(f32[8,64,4096]{2,0,1:T(8,128)} %get-tuple-element.15) | data formatting | bytes 16777216 | tf_op jit(solution)/shard_map/add | solution.py:144
  237.2 9.8 %reshape.133 = f32[2,4,16,4,4096]{4,1,0,3,2:T(4,128)} reshape(f32[8,64,4096]{2,0,1:T(8,128)} %get-tuple-element.17) | data formatting | bytes 16777216 | tf_op jit(solution)/shard_map/reshape | solution.py:133
  247.0 9.8 %sub.118 = f32[2,4,16,4,4096]{4,1,0,3,2:T(4,128)} reshape(f32[8,64,4096]{2,0,1:T(8,128)} %get-tuple-element.16) | data formatting | bytes 16777216 | tf_op jit(solution)/shard_map/sub | solution.py:153
  264.4 3.6 reshape.128
  268.0 43.3 %fusion = f32[4,2,64,4096]{3,2,1,0:T(8,128)} fusion(f32[4,2,64,1026]{3,2,1,0:T(8,128)} %reshape.128, s32[4096]{0:T(1024)S(1)} %copy-done.9, s32[4096]{0:T(1024)} %get-tuple-element.43, s32[4096]{0:T(1024)S(1)} %copy-done.7, s32[4096]{0:T(1024)S(1)} %copy-done.8, pred[4096]{0:T(1024)(128)(4,1)S(1)} %get-tuple-element.45, ...), kind=kOutput, calls=%fused_computation.5 | convolution fusion | flops 25912590336 | bytes 10563584 | tf_op jit(solution)/shard_map/fqyj,jx->fqyx/dot_general | solution.py:127
  311.3 8.4 %fusion.192 = (f32[1,2,64,4096]{3,2,1,0:T(8,128)}, f32[2,64,4096]{2,1,0:T(8,128)S(1)}, f32[2,64,4096]{2,1,0:T(8,128)}, f32[2,64,4096]{2,1,0:T(8,128)}, f32[1,2,6...) fusion(f32[4,2,64,4096]{3,2,1,0:T(8,128)} %fusion), kind=kLoop, calls=%fused_computation.237 | loop fusion | bytes 23068672 | tf_op jit(solution)/shard_map/slice | solution.py:158
  322.7 6.9 %mul.435 = f32[2,4,64,4096]{3,1,0,2:T(4,128)} broadcast(f32[2,64,4096]{2,0,1:T(2,128)} %copy.103), dimensions={0,2,3} | broadcast | bytes 10485760 | tf_op jit(solution)/shard_map/mul | solution.py:153
  329.6 10.0 %mul.436 = f32[8,64,4096]{2,0,1:T(8,128)} reshape(f32[2,4,64,4096]{3,1,0,2:T(4,128)} %mul.435) | data formatting | bytes 16777216 | tf_op jit(solution)/shard_map/mul | solution.py:153
  339.6 4.5 copy.104
  344.1 7.0 %mul.439 = f32[2,4,64,4096]{3,1,0,2:T(4,128)} broadcast(f32[2,64,4096]{2,0,1:T(2,128)} %copy.104), dimensions={0,2,3} | broadcast | bytes 10485760 | tf_op jit(solution)/shard_map/mul | solution.py:154
  351.0 10.0 %mul.440 = f32[8,64,4096]{2,0,1:T(8,128)} reshape(f32[2,4,64,4096]{3,1,0,2:T(4,128)} %mul.439) | data formatting | bytes 16777216 | tf_op jit(solution)/shard_map/mul | solution.py:154
  361.1 4.5 copy.105
  365.6 7.0 %mul.444 = f32[2,4,64,4096]{3,1,0,2:T(4,128)} broadcast(f32[2,64,4096]{2,0,1:T(2,128)} %copy.105), dimensions={0,2,3} | broadcast | bytes 10485760 | tf_op jit(solution)/shard_map/mul | solution.py:155
  372.6 10.1 %mul.445 = f32[8,64,4096]{2,0,1:T(8,128)} reshape(f32[2,4,64,4096]{3,1,0,2:T(4,128)} %mul.444) | data formatting | bytes 16777216 | tf_op jit(solution)/shard_map/mul | solution.py:155
  382.7 47.6 %multiply_add_fusion.2 = (f32[8,64,4096]{2,0,1:T(8,128)}, f32[8,64,4096]{2,0,1:T(8,128)}, f32[8,64,4096]{2,0,1:T(8,128)}) fusion(f32[8,64,4096]{2,0,1:T(8,128)} %copy.106, f32[8,64,4096]{2,0,1:T(8,128)} %mul.445, f32[8,64,4096]{2,0,1:T(8,128)} %mul.440, f32[8,64,4096]{2,0,1:T(8,128)} %mul.436, f32[8]{0:T(128)S(1)} %copy-done.12, ...), kind=kLoop, calls=%fused_computation.52 | loop fusion | flops 62914560 | bytes 71641280 | tf_op jit(solution)/shard_map/add | solution.py:157
  430.3 9.7 %reshape.130 = f32[2,4,16,4,4096]{4,1,0,3,2:T(4,128)} reshape(f32[8,64,4096]{2,0,1:T(8,128)} %get-tuple-element.10) | data formatting | bytes 16777216 | tf_op jit(solution)/shard_map/reshape | solution.py:133
  440.1 10.0 %reshape.131 = f32[2,4,16,4,4096]{4,1,0,3,2:T(4,128)} reshape(f32[8,64,4096]{2,0,1:T(8,128)} %get-tuple-element.9) | data formatting | bytes 16777216 | tf_op jit(solution)/shard_map/reshape | solution.py:133
  450.1 3.4 copy.129
  459.8 26.2 %subtract_reduce_fusion = f32[2,16,4096]{2,0,1:T(2,128)S(1)} fusion(f32[2,4,16,4,4096]{4,1,0,3,2:T(4,128)} %reshape.132, f32[2,4,16,4,4096]{4,1,0,3,2:T(4,128)} %reshape.133, f32[2,4,16,4,4096]{4,1,0,3,2:T(4,128)} %reshape.130, f32[2,4,16,4,4096]{4,1,0,3,2:T(4,128)} %reshape.131, f32[2,4,16,4,4096]{4,1,0,3,2:T(4,128)} %sub.118, ...), kind=kLoop, calls=%fused_computation.51 | loop fusion | flops 41811968 | bytes 67633184 | tf_op jit(solution)/shard_map/reduce_sum | solution.py:159
  485.9 11.8 %fusion.15 = f32[2,16,1024]{2,1,0:T(8,128)S(1)} fusion(s32[4096]{0:T(1024)S(1)} %copy-done.7, s32[4096]{0:T(1024)S(1)} %copy-done.8, pred[4096]{0:T(1024)(128)(4,1)S(1)} %get-tuple-element.46, f32[2,16,4096]{2,0,1:T(2,128)S(1)} %subtract_reduce_fusion), kind=kOutput, calls=%fused_computation.20 | convolution fusion | flops 1623326720 | bytes 692224 | tf_op jit(solution)/shard_map/qyx,xc->qyc/dot_general | solution.py:162
  498.5 4.9 all-to-all-start.3
  503.7 5.9 all-to-all-done.3
  513.6 8.0 %copy.118 = f32[2,2,4,4096]{2,1,0,3:T(2,128)} copy(f32[2,2,4,4096]{3,2,1,0:T(4,128)S(1)} %pad_maximum_fusion.14) | data formatting | bytes 524288 | tf_op jit(solution)/shard_map/stack | solution.py:169
  521.6 14.3 %reshape.145 = f32[4,1,16384]{2,1,0:T(1,128)S(1)} reshape(f32[4096,2,2,4]{3,2,1,0:T(2,128)} %bitcast.150) | data formatting | bytes 524288
  535.9 11.1 %all_to_all.68 = f32[4,1,16384]{2,1,0:T(1,128)S(1)} all-to-all(f32[4,1,16384]{2,1,0:T(1,128)S(1)} %reshape.145), channel_id=1, replica_groups=mesh['grp'=4,'gx'=4,'gy'=2] {'gx'}, dimensions={0} | all-to-all | bytes 524288 | tf_op jit(solution)/shard_map/all_to_all | solution.py:168
  548.4 16.5 %reshape.146 = f32[4096,2,2,4]{3,2,1,0:T(2,128)} reshape(f32[4,16384]{1,0:T(4,128)S(1)} %reduce.1) | data formatting | bytes 524288
  564.9 10.6 %copy.119 = f32[2,2,4,4,1024]{4,3,2,1,0:T(4,128)S(1)} copy(f32[2,2,4,4,1024]{3,1,0,4,2:T(2,128)} %bitcast.151) | data formatting | bytes 524288 | tf_op jit(solution)/shard_map/all_to_all | solution.py:168
  577.6 11.7 %copy.120 = f32[8,64,4096]{2,1,0:T(8,128)} copy(f32[8,64,4096]{2,0,1:T(8,128)} %get-tuple-element.8) | data formatting | bytes 16777216
  589.3 13.1 %all-gather.2.cloned.1.call-done = f32[2,8,16,1024]{3,2,1,0:T(8,128)} async-done(((f32[2,2,16,1024]{3,2,1,0:T(8,128)}), f32[2,8,16,1024]{3,2,1,0:T(8,128)}) %all-gather.2.cloned.1.call-update) | async-done | bytes 1048592 | tf_op jit(solution)/shard_map/all_gather | solution.py:171
  (107 shorter events, 59.9 us)
Async XLA Ops:
  10.0 59.5 %all-to-all-start = ((f32[2,8,16,1024]{3,1,0,2:T(8,128)}), f32[2,8,16,1024]{3,1,0,2:T(8,128)S(1)}, u32[]{:S(2)}, u32[]{:S(2)}) async-start(f32[2,8,16,1024]{3,1,0,2:T(8,128)} %bitcast.143), calls=%async_computation | async-start | bytes 2097152 | tf_op jit(solution)/shard_map/all_to_all | solution.py:115
  19.0 26.0 %collective-permute-start.1 = (f32[1,64,4096]{2,1,0:T(8,128)S(1)}, f32[1,64,4096]{2,1,0:T(8,128)S(1)}, u32[]{:S(2)}, u32[]{:S(2)}) collective-permute-start(f32[1,64,4096]{2,1,0:T(8,128)S(1)} %get-tuple-element.26), channel_id=1, source_target_pairs={{8,0},{16,8},{24,16},{0,24},{9,1},{17,9},{25,17},{1,25},{10,2},{18... | collective-permute-start | bytes 3145736 | tf_op jit(solution)/shard_map/ppermute | solution.py:20
  21.5 45.7 %collective-permute-start = (f32[1,64,4096]{2,1,0:T(8,128)}, f32[1,64,4096]{2,1,0:T(8,128)}, u32[]{:S(2)}, u32[]{:S(2)}) collective-permute-start(f32[1,64,4096]{2,1,0:T(8,128)} %get-tuple-element.25), channel_id=1, source_target_pairs={{0,8},{8,16},{16,24},{24,0},{1,9},{9,17},{17,25},{25,1},{2,10},{10... | collective-permute-start | bytes 3145736 | tf_op jit(solution)/shard_map/ppermute | solution.py:18
  33.1 9.9 %copy-start.11 = (f32[8]{0:T(128)S(1)}, f32[8]{0:T(128)}, u32[]{:S(2)}) copy-start(f32[8]{0:T(128)} %param.9) | copy-start | bytes 100
  43.8 34.0 %copy-start.5 = (f32[32,128]{1,0:T(8,128)}, f32[32,128]{1,0:T(8,128)S(1)}, u32[]{:S(2)}) copy-start(f32[32,128]{1,0:T(8,128)S(1)} %get-tuple-element.40) | copy-start | bytes 49156
  98.3 21.6 %all-to-all-start.1 = ((f32[4,1,32768]{2,1,0:T(1,128)}), f32[4,1,32768]{2,1,0:T(1,128)}, u32[]{:S(2)}, u32[]{:S(2)}) async-start(f32[4,1,32768]{2,1,0:T(1,128)} %reshape.143), calls=%async_computation.1 | async-start | bytes 1048576 | tf_op jit(solution)/shard_map/all_to_all | solution.py:117
  109.2 5.8 copy-start
  116.1 55.0 %collective-permute-start.2 = (f32[10,64,1]{2,0,1:T(8,128)}, f32[10,64,1]{2,0,1:T(8,128)S(1)}, u32[]{:S(2)}, u32[]{:S(2)}) collective-permute-start(f32[10,64,1]{2,0,1:T(8,128)} %get-tuple-element.13), channel_id=1, source_target_pairs={{2,0},{4,2},{6,4},{0,6},{3,1},{5,3},{7,5},{1,7},{10,8},{12,10},{14... | collective-permute-start | bytes 7688 | tf_op jit(solution)/shard_map/ppermute | solution.py:20
  119.9 51.2 %collective-permute-start.3 = (f32[10,64,1]{2,0,1:T(8,128)}, f32[10,64,1]{2,0,1:T(8,128)S(1)}, u32[]{:S(2)}, u32[]{:S(2)}) collective-permute-start(f32[10,64,1]{2,0,1:T(8,128)} %get-tuple-element.14), channel_id=1, source_target_pairs={{0,2},{2,4},{4,6},{6,0},{1,3},{3,5},{5,7},{7,1},{8,10},{10,12},{12... | collective-permute-start | bytes 7688 | tf_op jit(solution)/shard_map/ppermute | solution.py:18
  148.4 44.1 %all-to-all-start.2 = ((f32[4,2,16,1024]{3,2,1,0:T(8,128)}), f32[4,2,16,1024]{3,2,1,0:T(8,128)}, u32[]{:S(2)}, u32[]{:S(2)}) async-start(f32[4,2,16,1024]{3,2,1,0:T(8,128)} %reshape.127), calls=%async_computation.2 | async-start | bytes 1048576 | tf_op jit(solution)/shard_map/all_to_all | solution.py:118
  193.5 6.3 %collective-permute-start.6 = (f32[4,2,16,1]{3,2,1,0:T(8,128)S(1)}, f32[4,2,16,1]{3,2,1,0:T(8,128)S(1)}, u32[]{:S(2)}, u32[]{:S(2)}) collective-permute-start(f32[4,2,16,1]{3,2,1,0:T(8,128)S(1)} %get-tuple-element.38), channel_id=1, source_target_pairs={{0,2},{2,4},{4,6},{6,0},{1,3},{3,5},{5,7},{7,1},{8,10},{10,12},{12... | collective-permute-start | bytes 1544 | tf_op jit(solution)/shard_map/ppermute | solution.py:18
  193.7 6.0 collective-permute-start.7
  199.2 183.4 %collective-permute-start.4 = (f32[10,1,4098]{2,0,1:T(8,128)}, f32[10,1,4098]{2,0,1:T(8,128)S(1)}, u32[]{:S(2)}, u32[]{:S(2)}) collective-permute-start(f32[10,1,4098]{2,0,1:T(8,128)} %get-tuple-element.11), channel_id=1, source_target_pairs={{1,0},{0,1},{3,2},{2,3},{5,4},{4,5},{7,6},{6,7},{9,8},{8,9},{11,10... | collective-permute-start | bytes 491768 | tf_op jit(solution)/shard_map/ppermute | solution.py:20
  199.3 183.5 %collective-permute-start.5 = (f32[10,1,4098]{2,0,1:T(8,128)}, f32[10,1,4098]{2,0,1:T(8,128)}, u32[]{:S(2)}, u32[]{:S(2)}) collective-permute-start(f32[10,1,4098]{2,0,1:T(8,128)} %get-tuple-element.12), channel_id=1, source_target_pairs={{0,1},{1,0},{2,3},{3,2},{4,5},{5,4},{6,7},{7,6},{8,9},{9,8},{10,11... | collective-permute-start | bytes 491768 | tf_op jit(solution)/shard_map/ppermute | solution.py:18
  203.0 53.8 %collective-permute-start.8 = (f32[4,2,1,1026]{3,2,1,0:T(1,128)S(1)}, f32[4,2,1,1026]{3,2,1,0:T(1,128)S(1)}, u32[]{:S(2)}, u32[]{:S(2)}) collective-permute-start(f32[4,2,1,1026]{3,2,1,0:T(1,128)S(1)} %get-tuple-element.35), channel_id=1, source_target_pairs={{0,1},{1,0},{2,3},{3,2},{4,5},{5,4},{6,7},{7,6},{8,9},{9,8},{10,11... | collective-permute-start | bytes 98504 | tf_op jit(solution)/shard_map/ppermute | solution.py:18
  203.0 53.7 %collective-permute-start.9 = (f32[4,2,1,1026]{3,2,1,0:T(1,128)S(1)}, f32[4,2,1,1026]{3,2,1,0:T(1,128)}, u32[]{:S(2)}, u32[]{:S(2)}) collective-permute-start(f32[4,2,1,1026]{3,2,1,0:T(1,128)S(1)} %get-tuple-element.36), channel_id=1, source_target_pairs={{1,0},{0,1},{3,2},{2,3},{5,4},{4,5},{7,6},{6,7},{9,8},{8,9},{11,10... | collective-permute-start | bytes 98504 | tf_op jit(solution)/shard_map/ppermute | solution.py:20
  256.8 11.3 %copy-start.7 = (s32[4096]{0:T(1024)S(1)}, s32[4096]{0:T(1024)}, u32[]{:S(2)}) copy-start(s32[4096]{0:T(1024)} %get-tuple-element.41) | copy-start | bytes 49156
  256.8 11.3 %copy-start.8 = (s32[4096]{0:T(1024)S(1)}, s32[4096]{0:T(1024)}, u32[]{:S(2)}) copy-start(s32[4096]{0:T(1024)} %get-tuple-element.44) | copy-start | bytes 49156
  256.8 11.3 %copy-start.9 = (s32[4096]{0:T(1024)S(1)}, s32[4096]{0:T(1024)}, u32[]{:S(2)}) copy-start(s32[4096]{0:T(1024)} %get-tuple-element.42) | copy-start | bytes 49156
  372.5 10.2 %copy-start.12 = (f32[8]{0:T(128)S(1)}, f32[8]{0:T(128)}, u32[]{:S(2)}) copy-start(f32[8]{0:T(128)} %param.9) | copy-start | bytes 100
  440.1 13.4 %copy-start.3 = (f32[1,2,64,4096]{3,2,1,0:T(8,128)S(1)}, f32[1,2,64,4096]{3,2,1,0:T(8,128)}, u32[]{:S(2)}) copy-start(f32[1,2,64,4096]{3,2,1,0:T(8,128)} %get-tuple-element.24) | copy-start | bytes 6291460
  450.1 5.0 copy-start.2
  450.1 6.7 %copy-start.1 = (f32[1,2,64,4096]{3,2,1,0:T(8,128)S(1)}, f32[1,2,64,4096]{3,2,1,0:T(8,128)}, u32[]{:S(2)}) copy-start(f32[1,2,64,4096]{3,2,1,0:T(8,128)} %get-tuple-element.22) | copy-start | bytes 6291460
  450.1 9.6 %slice-start = ((s8[8388608]{0:T(1024)(128)(4,1)}), s8[4194304]{0:T(1024)(128)(4,1)S(1)}, s32[]{:S(2)}) async-start(s8[8388608]{0:T(1024)(128)(4,1)} %bitcast.146), calls=%async_computation.6 | async-start | bytes 8388608
  450.1 9.6 %copy-start.10 = (f32[2,4]{1,0:T(2,128)S(1)}, f32[2,4]{1,0:T(2,128)}, u32[]{:S(2)}) copy-start(f32[2,4]{1,0:T(2,128)} %mul.460) | copy-start | bytes 100
  455.1 4.6 slice-start.1
  485.9 24.5 %copy-start.6 = (f32[32,128]{1,0:T(8,128)S(1)}, f32[32,128]{1,0:T(8,128)}, u32[]{:S(2)}) copy-start(f32[32,128]{1,0:T(8,128)} %copy-done.5) | copy-start | bytes 49156
  498.5 11.1 %all-to-all-start.3 = ((f32[2,16,1024]{2,0,1:T(2,128)}), f32[2,16,1024]{2,0,1:T(2,128)S(1)}, u32[]{:S(2)}, u32[]{:S(2)}) async-start(f32[2,16,1024]{2,0,1:T(2,128)} %copy.114), calls=%async_computation.3 | async-start | bytes 262144 | tf_op jit(solution)/shard_map/all_to_all | solution.py:166
  503.4 99.0 %all-gather.2.cloned.1.call-start = ((), (), s32[]{:S(2)}) async-start(), calls=%async_computation.5 | async-start | bytes 1310720 | tf_op jit(solution)/shard_map/all_gather | solution.py:171
  577.6 24.9 %copy-start.4 = (f32[1,2,8,16,1024]{4,3,2,1,0:T(8,128)S(1)}, f32[1,2,8,16,1024]{4,3,2,1,0:T(8,128)}, u32[]{:S(2)}) copy-start(f32[1,2,8,16,1024]{4,3,2,1,0:T(8,128)} %param.5) | copy-start | bytes 3145732
Sparse Core Ops, SparseCore 0:
  576.4 26.0 all-gather.1
where the time goes:
time: 621 us; the launch traced here: 612 us
  local copies, waits for them, and re-layouts  322 us (52%)
  other arithmetic  127 us (20%)
  matrix products  63.9 us (10%)
  waiting for transfers between devices  40.1 us (6%)
  starting transfers between devices  32.1 us (5%)
  between operations  16 us (3%)
  blocking collectives  11.1 us (2%)
    unnamed x37, local copies, waits for them, and re-layouts  89.2 us
    reshape x5, local copies, waits for them, and re-layouts, levels(): return piece.reshape((quarter, RATIO) + piece.shape[1:])  49.2 us
    add x1, other arithmetic, per_device(): updated = centre + fine_step * (spread - advection)  47.6 us
    dot_general x1, matrix products, per_device(): jnp.einsum('fqyj,jx->fqyx', along_y, spread_table(width), precision=lax.P...  43.3 us
    reduce_sum x1, other arithmetic, per_device(): buoyancy.reshape(quarter, RATIO, row_count, RATIO, width * RATIO)  26.2 us
    mul x4, local copies, waits for them, and re-layouts, per_device(): velocity[2] * (upper_cells - lower_cells) * 0.5  24.6 us
    add x1, other arithmetic, per_device(): east_cells + west_cells + north_cells + south_cells + upper_cells  23.8 us
    concatenate x2, local copies, waits for them, and re-layouts, extended(): jnp.concatenate([lax.ppermute(tail, axis, [(i, (i + 1) % count) for i in...  23.5 us
  transfers between devices with their start and end apart: 15, of which 3 were waited for; matrix products, arithmetic and copies ran while one was open for 49% of the time, Pallas kernels for 0%

commit v1 on v0

--- a/solution.py
+++ b/solution.py
@@ -114,7 +114,10 @@
     quarter = planes // groups
     pencil = lax.all_to_all(coarse_modes[0], "gx", split_axis=2, concat_axis=3, tiled=True)
     physical = fourier_lines(pencil[0], pencil[1], 1.0, False)
-    blocks = lax.all_to_all(physical, "gx", split_axis=2, concat_axis=1, tiled=True)
+    blocks = jnp.concatenate(
+        lax.all_to_all(jnp.stack(jnp.split(physical, lax.axis_size("gx"), axis=2)), "gx", 0, 0),
+        axis=1,
+    )
     received = lax.all_to_all(
         blocks.reshape(groups, quarter, row_count, width),
         "grp",

time: 621 us -> 583 us (0.939)
  local copies, waits for them, and re-layouts: 322 us -> 288 us
    unnamed x37 -> x35, local copies, waits for them, and re-layouts: 89.2 us -> 62.8 us
    all_to_all x2 -> x0, local copies, waits for them, and re-layouts: 8.25 us -> none  [per_device(): lax.all_to_all(physical, 'gx', split_axis=2, concat_axis=1, tiled=True)]
  transfers between devices with their start and end apart: 15 -> 15, of which waited for: 3 -> 3; matrix products, arithmetic and copies ran while one was open for 49% -> 48% of each run, Pallas kernels for 0% -> 0%
where the time goes in v1:
time: 583 us; the launch traced here: 574 us
  local copies, waits for them, and re-layouts  288 us (49%)
  other arithmetic  123 us (21%)
  matrix products  63.7 us (11%)
  waiting for transfers between devices  40.1 us (7%)
  starting transfers between devices  32.2 us (6%)
  between operations  16.2 us (3%)
  blocking collectives  11.1 us (2%)
    unnamed x35, local copies, waits for them, and re-layouts  62.8 us
    reshape x5, local copies, waits for them, and re-layouts, levels(): return piece.reshape((quarter, RATIO) + piece.shape[1:])  49.3 us
    add x1, other arithmetic, per_device(): updated = centre + fine_step * (spread - advection)  47.7 us
    dot_general x1, matrix products, per_device(): jnp.einsum('fqyj,jx->fqyx', along_y, spread_table(width), precision=lax.P...  43.1 us
    reduce_sum x1, other arithmetic, per_device(): buoyancy.reshape(quarter, RATIO, row_count, RATIO, width * RATIO)  25.9 us
    mul x4, local copies, waits for them, and re-layouts, per_device(): velocity[2] * (upper_cells - lower_cells) * 0.5  24.8 us
    add x1, other arithmetic, per_device(): east_cells + west_cells + north_cells + south_cells + upper_cells  23.7 us
    concatenate x2, local copies, waits for them, and re-layouts, extended(): jnp.concatenate([lax.ppermute(tail, axis, [(i, (i + 1) % count) for i in...  23.5 us
  transfers between devices with their start and end apart: 15, of which 3 were waited for; matrix products, arithmetic and copies ran while one was open for 48% of the time, Pallas kernels for 0%

profile of v1, /device:TPU:0, one launch (start us, length us, event | category | flops | bytes accessed | tf_op | source)
XLA Modules:
  0.0 574.0 jit_solution(10951191359580573830)
XLA Ops:
  7.2 2.8 copy.139
  10.0 6.3 %all-to-all-start = ((f32[2,8,16,1024]{3,1,0,2:T(8,128)}), f32[2,8,16,1024]{3,1,0,2:T(8,128)S(1)}, u32[]{:S(2)}, u32[]{:S(2)}) async-start(f32[2,8,16,1024]{3,1,0,2:T(8,128)} %bitcast.154), calls=%async_computation | async-start | bytes 2097152 | tf_op jit(solution)/shard_map/all_to_all | solution.py:115
  16.3 2.7 fusion.193
  21.5 11.6 %copy.106 = f32[8,64,4096]{2,0,1:T(8,128)} copy(f32[8,64,4096]{2,1,0:T(8,128)} %param.6) | data formatting | bytes 16777216 | tf_op args[1]
  33.1 10.0 %reshape.128 = f32[2,4,16,4,4096]{4,3,2,1,0:T(4,128)} reshape(f32[8,64,4096]{2,1,0:T(8,128)} %param.6) | data formatting | bytes 16777216 | tf_op jit(solution)/shard_map/reshape | solution.py:136
  46.2 21.0 %collective-permute-done = f32[1,64,4096]{2,1,0:T(8,128)} collective-permute-done((f32[1,64,4096]{2,1,0:T(8,128)}, f32[1,64,4096]{2,1,0:T(8,128)}, u32[]{:S(2)}, u32[]{:S(2)}) %collective-permute-start) | collective-permute-done | bytes 1048608 | tf_op jit(solution)/shard_map/ppermute | solution.py:18
  84.1 4.8 all-to-all-start.1
  88.9 5.6 pad_maximum_fusion
  94.6 5.8 %copy-done = f32[10,64,4096]{2,0,1:T(8,128)} copy-done((f32[10,64,4096]{2,0,1:T(8,128)}, f32[10,64,4096]{2,0,1:T(8,128)S(1)}, u32[]{:S(2)}) %copy-start) | copy-done | bytes 10485784
  101.4 3.8 collective-permute-start.2
  109.5 4.6 all-to-all-start.2
  114.2 8.8 %pad_maximum_fusion.2 = f32[8,64,4096]{2,0,1:T(8,128)} fusion(f32[1,64,4096]{2,0,1:T(1,128)S(1)} %copy.90, f32[8,64,4096]{2,0,1:T(8,128)} %copy.106), kind=kLoop, calls=%fused_computation.38 | loop fusion | flops 2097152 | bytes 17825792 | tf_op jit(solution)/shard_map/concatenate | solution.py:16
  122.9 9.8 %reshape.131 = f32[2,4,16,4,4096]{4,1,0,3,2:T(4,128)} reshape(f32[8,64,4096]{2,0,1:T(8,128)} %pad_maximum_fusion.2) | data formatting | bytes 16777216 | tf_op jit(solution)/shard_map/reshape | solution.py:136
  132.7 21.5 %concatenate.38 = f32[10,64,4098]{2,0,1:T(8,128)} concatenate(f32[10,64,1]{2,0,1:T(8,128)S(1)} %collective-permute-done.3, f32[10,64,4096]{2,0,1:T(8,128)} %copy-done, f32[10,64,1]{2,0,1:T(8,128)S(1)} %collective-permute-done.2), dimensions={2} | concatenate | bytes 20981760 | tf_op jit(solution)/shard_map/concatenate | solution.py:16
  155.4 3.7 collective-permute-start.7
  165.2 23.7 %fusion.36 = (f32[8,64,4096]{2,0,1:T(8,128)}, f32[8,64,4096]{2,0,1:T(8,128)}, f32[8,64,4096]{2,0,1:T(8,128)}) fusion(f32[10,64,1]{2,0,1:T(8,128)S(1)} %collective-permute-done.2, f32[1,64,4096]{2,0,1:T(1,128)S(1)} %copy.90, f32[8,64,4096]{2,0,1:T(8,128)} %copy.106, f32[1,64,4096]{2,0,1:T(1,128)S(1)} %copy.88, f32[10,64,1]{2,0,1:T(8,128)S(1)} %collective-permute-done.3), kind=kLoop, calls=%fused_computation.54 | loop fusion | flops 18874368 | bytes 35656704 | tf_op jit(solution)/shard_map/add | solution.py:147
  188.9 9.9 %add.235 = f32[2,4,16,4,4096]{4,1,0,3,2:T(4,128)} reshape(f32[8,64,4096]{2,0,1:T(8,128)} %get-tuple-element.15) | data formatting | bytes 16777216 | tf_op jit(solution)/shard_map/add | solution.py:147
  198.8 9.8 %reshape.132 = f32[2,4,16,4,4096]{4,1,0,3,2:T(4,128)} reshape(f32[8,64,4096]{2,0,1:T(8,128)} %get-tuple-element.17) | data formatting | bytes 16777216 | tf_op jit(solution)/shard_map/reshape | solution.py:136
  208.5 9.8 %sub.118 = f32[2,4,16,4,4096]{4,1,0,3,2:T(4,128)} reshape(f32[8,64,4096]{2,0,1:T(8,128)} %get-tuple-element.16) | data formatting | bytes 16777216 | tf_op jit(solution)/shard_map/sub | solution.py:156
  222.7 3.3 pad_maximum_fusion.11
  226.0 3.6 reshape.127
  229.6 43.1 %fusion = f32[4,2,64,4096]{3,2,1,0:T(8,128)} fusion(f32[4,2,64,1026]{3,2,1,0:T(8,128)} %reshape.127, s32[4096]{0:T(1024)S(1)} %copy-done.9, s32[4096]{0:T(1024)} %get-tuple-element.47, s32[4096]{0:T(1024)S(1)} %copy-done.7, s32[4096]{0:T(1024)S(1)} %copy-done.8, pred[4096]{0:T(1024)(128)(4,1)S(1)} %get-tuple-element.49, ...), kind=kOutput, calls=%fused_computation.5 | convolution fusion | flops 25912590336 | bytes 10563584 | tf_op jit(solution)/shard_map/fqyj,jx->fqyx/dot_general | solution.py:130
  272.6 8.4 %fusion.192 = (f32[1,2,64,4096]{3,2,1,0:T(8,128)}, f32[2,64,4096]{2,1,0:T(8,128)S(1)}, f32[2,64,4096]{2,1,0:T(8,128)}, f32[2,64,4096]{2,1,0:T(8,128)}, f32[1,2,6...) fusion(f32[4,2,64,4096]{3,2,1,0:T(8,128)} %fusion), kind=kLoop, calls=%fused_computation.242 | loop fusion | bytes 23068672 | tf_op jit(solution)/shard_map/slice | solution.py:161
  281.0 2.9 copy.103
  284.0 7.0 %mul.435 = f32[2,4,64,4096]{3,1,0,2:T(4,128)} broadcast(f32[2,64,4096]{2,0,1:T(2,128)} %copy.103), dimensions={0,2,3} | broadcast | bytes 10485760 | tf_op jit(solution)/shard_map/mul | solution.py:156
  290.9 10.0 %mul.436 = f32[8,64,4096]{2,0,1:T(8,128)} reshape(f32[2,4,64,4096]{3,1,0,2:T(4,128)} %mul.435) | data formatting | bytes 16777216 | tf_op jit(solution)/shard_map/mul | solution.py:156
  300.9 4.5 copy.104
  305.4 7.0 %mul.439 = f32[2,4,64,4096]{3,1,0,2:T(4,128)} broadcast(f32[2,64,4096]{2,0,1:T(2,128)} %copy.104), dimensions={0,2,3} | broadcast | bytes 10485760 | tf_op jit(solution)/shard_map/mul | solution.py:157
  312.4 10.0 %mul.440 = f32[8,64,4096]{2,0,1:T(8,128)} reshape(f32[2,4,64,4096]{3,1,0,2:T(4,128)} %mul.439) | data formatting | bytes 16777216 | tf_op jit(solution)/shard_map/mul | solution.py:157
  322.4 4.5 copy.105
  327.0 7.0 %mul.444 = f32[2,4,64,4096]{3,1,0,2:T(4,128)} broadcast(f32[2,64,4096]{2,0,1:T(2,128)} %copy.105), dimensions={0,2,3} | broadcast | bytes 10485760 | tf_op jit(solution)/shard_map/mul | solution.py:158
  333.9 10.4 %mul.445 = f32[8,64,4096]{2,0,1:T(8,128)} reshape(f32[2,4,64,4096]{3,1,0,2:T(4,128)} %mul.444) | data formatting | bytes 16777216 | tf_op jit(solution)/shard_map/mul | solution.py:158
  344.3 47.7 %multiply_add_fusion.2 = (f32[8,64,4096]{2,0,1:T(8,128)}, f32[8,64,4096]{2,0,1:T(8,128)}, f32[8,64,4096]{2,0,1:T(8,128)}) fusion(f32[8,64,4096]{2,0,1:T(8,128)} %copy.106, f32[8,64,4096]{2,0,1:T(8,128)} %mul.445, f32[8,64,4096]{2,0,1:T(8,128)} %mul.440, f32[8,64,4096]{2,0,1:T(8,128)} %mul.436, f32[8]{0:T(128)S(1)} %copy-done.12, ...), kind=kLoop, calls=%fused_computation.52 | loop fusion | flops 62914560 | bytes 71641280 | tf_op jit(solution)/shard_map/add | solution.py:160
  392.0 9.7 %reshape.129 = f32[2,4,16,4,4096]{4,1,0,3,2:T(4,128)} reshape(f32[8,64,4096]{2,0,1:T(8,128)} %get-tuple-element.10) | data formatting | bytes 16777216 | tf_op jit(solution)/shard_map/reshape | solution.py:136
  401.7 10.0 %reshape.130 = f32[2,4,16,4,4096]{4,1,0,3,2:T(4,128)} reshape(f32[8,64,4096]{2,0,1:T(8,128)} %get-tuple-element.9) | data formatting | bytes 16777216 | tf_op jit(solution)/shard_map/reshape | solution.py:136
  411.7 3.4 copy.128
  418.4 2.9 copy.131
  421.3 25.9 %subtract_reduce_fusion = f32[2,16,4096]{2,0,1:T(2,128)S(1)} fusion(f32[2,4,16,4,4096]{4,1,0,3,2:T(4,128)} %reshape.131, f32[2,4,16,4,4096]{4,1,0,3,2:T(4,128)} %reshape.132, f32[2,4,16,4,4096]{4,1,0,3,2:T(4,128)} %reshape.129, f32[2,4,16,4,4096]{4,1,0,3,2:T(4,128)} %reshape.130, f32[2,4,16,4,4096]{4,1,0,3,2:T(4,128)} %sub.118, ...), kind=kLoop, calls=%fused_computation.51 | loop fusion | flops 41811968 | bytes 67633184 | tf_op jit(solution)/shard_map/reduce_sum | solution.py:162
  447.3 11.8 %fusion.15 = f32[2,16,1024]{2,1,0:T(8,128)S(1)} fusion(s32[4096]{0:T(1024)S(1)} %copy-done.7, s32[4096]{0:T(1024)S(1)} %copy-done.8, pred[4096]{0:T(1024)(128)(4,1)S(1)} %get-tuple-element.50, f32[2,16,4096]{2,0,1:T(2,128)S(1)} %subtract_reduce_fusion), kind=kOutput, calls=%fused_computation.20 | convolution fusion | flops 1623326720 | bytes 692224 | tf_op jit(solution)/shard_map/qyx,xc->qyc/dot_general | solution.py:165
  459.8 4.9 all-to-all-start.3
  465.1 5.8 %all-to-all-done.3 = f32[2,16,1024]{2,0,1:T(2,128)S(1)} async-done(((f32[2,16,1024]{2,0,1:T(2,128)}), f32[2,16,1024]{2,0,1:T(2,128)S(1)}, u32[]{:S(2)}, u32[]{:S(2)}) %all-to-all-start.3) | async-done | bytes 131104 | tf_op jit(solution)/shard_map/all_to_all | solution.py:169
  474.9 8.0 %copy.118 = f32[2,2,4,4096]{2,1,0,3:T(2,128)} copy(f32[2,2,4,4096]{3,2,1,0:T(4,128)S(1)} %pad_maximum_fusion.15) | data formatting | bytes 524288 | tf_op jit(solution)/shard_map/stack | solution.py:172
  482.9 14.3 %reshape.142 = f32[4,1,16384]{2,1,0:T(1,128)S(1)} reshape(f32[4096,2,2,4]{3,2,1,0:T(2,128)} %bitcast.159) | data formatting | bytes 524288
  497.2 11.1 %all_to_all.58 = f32[4,1,16384]{2,1,0:T(1,128)S(1)} all-to-all(f32[4,1,16384]{2,1,0:T(1,128)S(1)} %reshape.142), channel_id=1, replica_groups=mesh['grp'=4,'gx'=4,'gy'=2] {'gx'}, dimensions={0} | all-to-all | bytes 524288 | tf_op jit(solution)/shard_map/all_to_all | solution.py:171
  510.2 16.5 %reshape.143 = f32[4096,2,2,4]{3,2,1,0:T(2,128)} reshape(f32[4,16384]{1,0:T(4,128)S(1)} %reduce) | data formatting | bytes 524288
  526.7 10.6 %copy.119 = f32[2,2,4,4,1024]{4,3,2,1,0:T(4,128)S(1)} copy(f32[2,2,4,4,1024]{3,1,0,4,2:T(2,128)} %bitcast.160) | data formatting | bytes 524288 | tf_op jit(solution)/shard_map/all_to_all | solution.py:171
  539.5 11.7 %copy.120 = f32[8,64,4096]{2,1,0:T(8,128)} copy(f32[8,64,4096]{2,0,1:T(8,128)} %get-tuple-element.8) | data formatting | bytes 16777216
  551.2 13.2 %all-gather.2.cloned.1.call-done = f32[2,8,16,1024]{3,2,1,0:T(8,128)} async-done(((f32[2,2,16,1024]{3,2,1,0:T(8,128)}), f32[2,8,16,1024]{3,2,1,0:T(8,128)}) %all-gather.2.cloned.1.call-update) | async-done | bytes 1048592 | tf_op jit(solution)/shard_map/all_gather | solution.py:174
  (107 shorter events, 52.8 us)
Async XLA Ops:
  10.0 59.5 %all-to-all-start = ((f32[2,8,16,1024]{3,1,0,2:T(8,128)}), f32[2,8,16,1024]{3,1,0,2:T(8,128)S(1)}, u32[]{:S(2)}, u32[]{:S(2)}) async-start(f32[2,8,16,1024]{3,1,0,2:T(8,128)} %bitcast.154), calls=%async_computation | async-start | bytes 2097152 | tf_op jit(solution)/shard_map/all_to_all | solution.py:115
  19.1 26.1 %collective-permute-start.1 = (f32[1,64,4096]{2,1,0:T(8,128)S(1)}, f32[1,64,4096]{2,1,0:T(8,128)S(1)}, u32[]{:S(2)}, u32[]{:S(2)}) collective-permute-start(f32[1,64,4096]{2,1,0:T(8,128)S(1)} %get-tuple-element.26), channel_id=1, source_target_pairs={{8,0},{16,8},{24,16},{0,24},{9,1},{17,9},{25,17},{1,25},{10,2},{18... | collective-permute-start | bytes 3145736 | tf_op jit(solution)/shard_map/ppermute | solution.py:20
  21.5 45.7 %collective-permute-start = (f32[1,64,4096]{2,1,0:T(8,128)}, f32[1,64,4096]{2,1,0:T(8,128)}, u32[]{:S(2)}, u32[]{:S(2)}) collective-permute-start(f32[1,64,4096]{2,1,0:T(8,128)} %get-tuple-element.25), channel_id=1, source_target_pairs={{0,8},{8,16},{16,24},{24,0},{1,9},{9,17},{17,25},{25,1},{2,10},{10... | collective-permute-start | bytes 3145736 | tf_op jit(solution)/shard_map/ppermute | solution.py:18
  33.1 10.0 %copy-start.11 = (f32[8]{0:T(128)S(1)}, f32[8]{0:T(128)}, u32[]{:S(2)}) copy-start(f32[8]{0:T(128)} %param.9) | copy-start | bytes 100
  43.9 34.0 %copy-start.5 = (f32[32,128]{1,0:T(8,128)}, f32[32,128]{1,0:T(8,128)S(1)}, u32[]{:S(2)}) copy-start(f32[32,128]{1,0:T(8,128)S(1)} %get-tuple-element.44) | copy-start | bytes 49156
  84.1 21.2 %all-to-all-start.1 = ((f32[4,8,4,1024]{3,1,2,0:T(8,128)}), f32[4,8,4,1024]{3,1,2,0:T(8,128)}, u32[]{:S(2)}, u32[]{:S(2)}) async-start(f32[4,8,4,1024]{3,1,2,0:T(8,128)} %pad_maximum_fusion.14), calls=%async_computation.1 | async-start | bytes 1048576 | tf_op jit(solution)/shard_map/all_to_all | solution.py:118
  94.5 5.8 %copy-start = (f32[10,64,4096]{2,0,1:T(8,128)}, f32[10,64,4096]{2,0,1:T(8,128)S(1)}, u32[]{:S(2)}) copy-start(f32[10,64,4096]{2,0,1:T(8,128)S(1)} %pad_maximum_fusion) | copy-start | bytes 31457284
  101.4 31.3 %collective-permute-start.2 = (f32[10,64,1]{2,0,1:T(8,128)}, f32[10,64,1]{2,0,1:T(8,128)S(1)}, u32[]{:S(2)}, u32[]{:S(2)}) collective-permute-start(f32[10,64,1]{2,0,1:T(8,128)} %get-tuple-element.13), channel_id=1, source_target_pairs={{2,0},{4,2},{6,4},{0,6},{3,1},{5,3},{7,5},{1,7},{10,8},{12,10},{14... | collective-permute-start | bytes 7688 | tf_op jit(solution)/shard_map/ppermute | solution.py:20
  105.3 27.4 %collective-permute-start.3 = (f32[10,64,1]{2,0,1:T(8,128)}, f32[10,64,1]{2,0,1:T(8,128)S(1)}, u32[]{:S(2)}, u32[]{:S(2)}) collective-permute-start(f32[10,64,1]{2,0,1:T(8,128)} %get-tuple-element.14), channel_id=1, source_target_pairs={{0,2},{2,4},{4,6},{6,0},{1,3},{3,5},{5,7},{7,1},{8,10},{10,12},{12... | collective-permute-start | bytes 7688 | tf_op jit(solution)/shard_map/ppermute | solution.py:18
  109.5 44.6 %all-to-all-start.2 = ((f32[4,2,16,1024]{3,2,1,0:T(8,128)}), f32[4,2,16,1024]{3,2,1,0:T(8,128)}, u32[]{:S(2)}, u32[]{:S(2)}) async-start(f32[4,2,16,1024]{3,2,1,0:T(8,128)} %copy.99), calls=%async_computation.2 | async-start | bytes 1048576 | tf_op jit(solution)/shard_map/all_to_all | solution.py:121
  155.1 6.3 %collective-permute-start.6 = (f32[4,2,16,1]{3,2,1,0:T(8,128)S(1)}, f32[4,2,16,1]{3,2,1,0:T(8,128)S(1)}, u32[]{:S(2)}, u32[]{:S(2)}) collective-permute-start(f32[4,2,16,1]{3,2,1,0:T(8,128)S(1)} %get-tuple-element.38), channel_id=1, source_target_pairs={{0,2},{2,4},{4,6},{6,0},{1,3},{3,5},{5,7},{7,1},{8,10},{10,12},{12... | collective-permute-start | bytes 1544 | tf_op jit(solution)/shard_map/ppermute | solution.py:18
  155.4 6.0 %collective-permute-start.7 = (f32[4,2,16,1]{3,2,1,0:T(8,128)S(1)}, f32[4,2,16,1]{3,2,1,0:T(8,128)S(1)}, u32[]{:S(2)}, u32[]{:S(2)}) collective-permute-start(f32[4,2,16,1]{3,2,1,0:T(8,128)S(1)} %get-tuple-element.37), channel_id=1, source_target_pairs={{2,0},{4,2},{6,4},{0,6},{3,1},{5,3},{7,5},{1,7},{10,8},{12,10},{14... | collective-permute-start | bytes 1544 | tf_op jit(solution)/shard_map/ppermute | solution.py:20
  160.9 183.4 %collective-permute-start.4 = (f32[10,1,4098]{2,0,1:T(8,128)}, f32[10,1,4098]{2,0,1:T(8,128)S(1)}, u32[]{:S(2)}, u32[]{:S(2)}) collective-permute-start(f32[10,1,4098]{2,0,1:T(8,128)} %get-tuple-element.11), channel_id=1, source_target_pairs={{1,0},{0,1},{3,2},{2,3},{5,4},{4,5},{7,6},{6,7},{9,8},{8,9},{11,10... | collective-permute-start | bytes 491768 | tf_op jit(solution)/shard_map/ppermute | solution.py:20
  160.9 183.4 %collective-permute-start.5 = (f32[10,1,4098]{2,0,1:T(8,128)}, f32[10,1,4098]{2,0,1:T(8,128)}, u32[]{:S(2)}, u32[]{:S(2)}) collective-permute-start(f32[10,1,4098]{2,0,1:T(8,128)} %get-tuple-element.12), channel_id=1, source_target_pairs={{0,1},{1,0},{2,3},{3,2},{4,5},{5,4},{6,7},{7,6},{8,9},{9,8},{10,11... | collective-permute-start | bytes 491768 | tf_op jit(solution)/shard_map/ppermute | solution.py:18
  164.6 53.7 %collective-permute-start.8 = (f32[4,2,1,1026]{3,2,1,0:T(1,128)S(1)}, f32[4,2,1,1026]{3,2,1,0:T(1,128)S(1)}, u32[]{:S(2)}, u32[]{:S(2)}) collective-permute-start(f32[4,2,1,1026]{3,2,1,0:T(1,128)S(1)} %get-tuple-element.35), channel_id=1, source_target_pairs={{0,1},{1,0},{2,3},{3,2},{4,5},{5,4},{6,7},{7,6},{8,9},{9,8},{10,11... | collective-permute-start | bytes 98504 | tf_op jit(solution)/shard_map/ppermute | solution.py:18
  164.7 53.6 %collective-permute-start.9 = (f32[4,2,1,1026]{3,2,1,0:T(1,128)S(1)}, f32[4,2,1,1026]{3,2,1,0:T(1,128)}, u32[]{:S(2)}, u32[]{:S(2)}) collective-permute-start(f32[4,2,1,1026]{3,2,1,0:T(1,128)S(1)} %get-tuple-element.36), channel_id=1, source_target_pairs={{1,0},{0,1},{3,2},{2,3},{5,4},{4,5},{7,6},{6,7},{9,8},{8,9},{11,10... | collective-permute-start | bytes 98504 | tf_op jit(solution)/shard_map/ppermute | solution.py:20
  218.3 11.3 %copy-start.7 = (s32[4096]{0:T(1024)S(1)}, s32[4096]{0:T(1024)}, u32[]{:S(2)}) copy-start(s32[4096]{0:T(1024)} %get-tuple-element.45) | copy-start | bytes 49156
  218.3 11.2 %copy-start.8 = (s32[4096]{0:T(1024)S(1)}, s32[4096]{0:T(1024)}, u32[]{:S(2)}) copy-start(s32[4096]{0:T(1024)} %get-tuple-element.48) | copy-start | bytes 49156
  218.3 11.2 %copy-start.9 = (s32[4096]{0:T(1024)S(1)}, s32[4096]{0:T(1024)}, u32[]{:S(2)}) copy-start(s32[4096]{0:T(1024)} %get-tuple-element.46) | copy-start | bytes 49156
  333.9 10.4 %copy-start.12 = (f32[8]{0:T(128)S(1)}, f32[8]{0:T(128)}, u32[]{:S(2)}) copy-start(f32[8]{0:T(128)} %param.9) | copy-start | bytes 100
  401.7 13.4 %copy-start.3 = (f32[1,2,64,4096]{3,2,1,0:T(8,128)S(1)}, f32[1,2,64,4096]{3,2,1,0:T(8,128)}, u32[]{:S(2)}) copy-start(f32[1,2,64,4096]{3,2,1,0:T(8,128)} %get-tuple-element.24) | copy-start | bytes 6291460
  411.7 5.0 copy-start.2
  411.7 6.7 %copy-start.1 = (f32[1,2,64,4096]{3,2,1,0:T(8,128)S(1)}, f32[1,2,64,4096]{3,2,1,0:T(8,128)}, u32[]{:S(2)}) copy-start(f32[1,2,64,4096]{3,2,1,0:T(8,128)} %get-tuple-element.22) | copy-start | bytes 6291460
  411.7 9.6 %slice-start = ((s8[8388608]{0:T(1024)(128)(4,1)}), s8[4194304]{0:T(1024)(128)(4,1)S(1)}, s32[]{:S(2)}) async-start(s8[8388608]{0:T(1024)(128)(4,1)} %bitcast.157), calls=%async_computation.6 | async-start | bytes 8388608
  411.7 9.6 %copy-start.10 = (f32[2,4]{1,0:T(2,128)S(1)}, f32[2,4]{1,0:T(2,128)}, u32[]{:S(2)}) copy-start(f32[2,4]{1,0:T(2,128)} %mul.460) | copy-start | bytes 100
  416.7 4.6 slice-start.1
  447.3 24.5 %copy-start.6 = (f32[32,128]{1,0:T(8,128)S(1)}, f32[32,128]{1,0:T(8,128)}, u32[]{:S(2)}) copy-start(f32[32,128]{1,0:T(8,128)} %copy-done.5) | copy-start | bytes 49156
  459.8 11.1 %all-to-all-start.3 = ((f32[2,16,1024]{2,0,1:T(2,128)}), f32[2,16,1024]{2,0,1:T(2,128)S(1)}, u32[]{:S(2)}, u32[]{:S(2)}) async-start(f32[2,16,1024]{2,0,1:T(2,128)} %copy.114), calls=%async_computation.3 | async-start | bytes 262144 | tf_op jit(solution)/shard_map/all_to_all | solution.py:169
  464.8 99.6 %all-gather.2.cloned.1.call-start = ((), (), s32[]{:S(2)}) async-start(), calls=%async_computation.5 | async-start | bytes 1310720 | tf_op jit(solution)/shard_map/all_gather | solution.py:174
  539.4 24.9 %copy-start.4 = (f32[1,2,8,16,1024]{4,3,2,1,0:T(8,128)S(1)}, f32[1,2,8,16,1024]{4,3,2,1,0:T(8,128)}, u32[]{:S(2)}) copy-start(f32[1,2,8,16,1024]{4,3,2,1,0:T(8,128)} %param.5) | copy-start | bytes 3145732
Sparse Core Ops, SparseCore 0:
  538.3 26.0 all-gather.1
